TPU v7x, 128 devices: a whole 4x4x4 slice. The times are simulated.
128 devices in a mesh: seq: 16 (over y_hi, z, core), tp: 8 (over y_lo, x).
Axes of the slice: x: 4, y: 4 (y_hi: 2, y_lo: 2; y = y_hi * 2 + y_lo), z: 4, core: 2. Of those that a mesh axis runs over, the one named last changes fastest.
Arguments:
- queries: bfloat16 [1024, 8192], P(None, 'tp'), may hold values from -80 to 80
- cache: bfloat16 [2, 16, 16384, 1024], P(None, None, 'seq', 'tp'), may hold values from -6 to 6
- draft_kv: bfloat16 [2, 1024, 1024], P(None, 'seq', 'tp'), may hold values from -9 to 9
- out_weight: bfloat16 [8192, 8192], P('tp', 'seq'), may hold values from -0.0625 to 0.0625
- lengths: int32 [16], replicated, may hold values from 1020 to 16376, as said below
- parents: int32 [16, 64], replicated, may hold values from -1 to 62, as said below
- path: int32 [16, 8], replicated, may hold values from 0 to 63, as said below
- accepted: int32 [16], replicated, may hold values from 1 to 8
Outputs:
- attn_out: bfloat16 [1024, 8192], P('tp', 'seq')
- new_cache: bfloat16 [2, 16, 16384, 1024], P(None, None, 'seq', 'tp')
Inputs may be any that keep to these rules, and one draw needn't show every extreme that they name: `lengths`: request r belongs to tenant t = r mod 4; a request of tenant t holds at most 16384 // 8 * 2 ** t - 8 tokens and at least half of that, and the first request of each tenant holds exactly that many. `parents`: node 0 is the root, with parent -1; every other node i has its parent among the nodes i - 7 to i - 1. `path`: for each request, the nodes of one branch of its tree, each the parent of the next, the last being node 63.
All inputs are finite; a program needn't handle non-finite values.
Results may differ from a plain program's by a relative error of at most 0.0051.
Values may be sent and summed in bfloat16 or wider, within the bound.
A program may use at most 192 MiB of HBM per device.

v0:
```python
import jax
import jax.numpy as jnp
from jax import lax
from jax.sharding import PartitionSpec as P

HEAD = 128
Q = 64
ACC = 8
masked_score = -1e30


def merged_2(array, axis, combine):
    everything = jax.tree.map(lambda part: lax.all_gather(part, axis), array)
    leading = jax.tree.map(lambda part: part[0], everything)

    def hop(k, so_far):
        return combine(so_far, jax.tree.map(lambda part: part[k], everything))

    return lax.fori_loop(1, lax.axis_size(axis), hop, leading)


def ancestors(parents):
    node_count = parents.shape[1]
    node_ids = jnp.arange(node_count, dtype=jnp.int32)
    step_map = (parents[:, :, None] == node_ids[None, None, :]).astype(jnp.float32)
    identity = jnp.broadcast_to(jnp.eye(node_count, dtype=jnp.float32), step_map.shape)
    reached = jnp.minimum(identity + step_map, 1.0)
    for doubling in range((node_count - 1).bit_length()):
        as_bits = reached.astype(jnp.bfloat16)
        squared = jnp.einsum("nij,njk->nik", as_bits, as_bits, preferred_element_type=jnp.float32)
        reached = jnp.minimum(squared, 1.0)
    return reached


def partial_block(query_rows, key_rows, value_rows, alive_mask):
    scores = jnp.einsum(
        "nqkge,npke->nqkgp", query_rows, key_rows, preferred_element_type=jnp.float32
    ) * HEAD ** (-0.5)
    masked = jnp.where(alive_mask, scores, masked_score)
    peak_score = jnp.max(masked, axis=-1)
    weights = jnp.where(alive_mask, jnp.exp(scores - peak_score[..., None]), 0.0)
    denominator = jnp.sum(weights, axis=-1)
    weighted = jnp.einsum(
        "nqkgp,npke->nqkge",
        weights.astype(jnp.bfloat16),
        value_rows,
        preferred_element_type=jnp.float32,
    )
    return (peak_score, denominator, weighted)


def join_flat(former, latter):
    peak_score = jnp.maximum(former[0], latter[0])
    weight_former = jnp.exp(former[0] - peak_score)
    weight_latter = jnp.exp(latter[0] - peak_score)
    row_count, head_count = peak_score.shape
    weighted = (
        former[2].reshape(row_count, head_count, -1) * weight_former[..., None]
        + latter[2].reshape(row_count, head_count, -1) * weight_latter[..., None]
    )
    return (
        peak_score,
        former[1] * weight_former + latter[1] * weight_latter,
        weighted.reshape(row_count, -1),
    )


def finish(query_flat, draft_rows, family, partials, kv_local):
    node_sets = family.shape[0]
    heads_local = query_flat.shape[1] // HEAD
    group_size = heads_local // kv_local
    reach = ancestors(family)
    query_rows = query_flat.reshape(node_sets, Q, kv_local, group_size, HEAD)
    key_rows = draft_rows[0].reshape(node_sets, Q, kv_local, HEAD)
    value_rows = draft_rows[1].reshape(node_sets, Q, kv_local, HEAD)
    draft_part = partial_block(query_rows, key_rows, value_rows, reach[:, :, None, None, :] > 0.5)
    row_count = node_sets * Q
    draft_part = (
        draft_part[0].reshape(row_count, heads_local),
        draft_part[1].reshape(row_count, heads_local),
        draft_part[2].reshape(row_count, heads_local * HEAD),
    )
    peak_score, denominator, weighted = join_flat(partials, draft_part)
    result = weighted.reshape(row_count, heads_local, HEAD) / denominator[..., None]
    return result.reshape(row_count, heads_local * HEAD).astype(jnp.bfloat16)


def select_rows(draft_rows, branch_path):
    node_sets = branch_path.shape[0]
    draft_table = draft_rows.reshape(2, node_sets, Q, draft_rows.shape[2])
    selector = (branch_path[:, :, None] == jnp.arange(Q, dtype=jnp.int32)[None, None, :]).astype(
        jnp.bfloat16
    )
    return jnp.einsum(
        "naq,xnqd->xnad", selector, draft_table, preferred_element_type=jnp.float32
    ).astype(jnp.bfloat16)


def local(queries, cache, draft_kv, out_weight, lengths, parents, path, accepted):
    seq_index = lax.axis_index("seq")
    requests = cache.shape[1]
    span_cache = cache.shape[2]
    kv_local = cache.shape[3] // HEAD
    heads_local = queries.shape[1] // HEAD
    group_size = heads_local // kv_local
    token_rows = requests * Q
    bundles = requests // 4
    positions = seq_index * span_cache + jnp.arange(span_cache, dtype=jnp.int32)
    alive_mask = positions[None, :] < lengths[:, None]
    query_blocks = queries.reshape(bundles, 4, Q, kv_local, group_size, HEAD)
    key_blocks = cache[0].reshape(bundles, 4, span_cache, kv_local, HEAD)
    value_blocks = cache[1].reshape(bundles, 4, span_cache, kv_local, HEAD)

    def cache_part(inputs):
        query_block, key_block, value_block, alive_block = inputs
        return partial_block(
            query_block, key_block, value_block, alive_block[:, None, None, None, :]
        )

    peak_score, denominator, weighted = lax.map(
        cache_part,
        (query_blocks, key_blocks, value_blocks, alive_mask.reshape(bundles, 4, span_cache)),
    )
    peak_score = peak_score.reshape(token_rows, heads_local)
    denominator = denominator.reshape(token_rows, heads_local)
    weighted = weighted.reshape(token_rows, heads_local * HEAD)
    drafts = lax.all_gather(draft_kv, "seq", axis=1, tiled=True)
    merged = merged_2((peak_score, denominator, weighted), "seq", join_flat)
    attended = finish(queries, drafts, parents, merged, kv_local)
    chosen = select_rows(drafts, path)
    attn_out = lax.psum_scatter(
        jnp.dot(attended, out_weight, preferred_element_type=jnp.float32),
        "tp",
        scatter_dimension=0,
        tiled=True,
    ).astype(jnp.bfloat16)
    offset = positions[None, :] - lengths[:, None]
    writable = (offset >= 0) & (offset < accepted[:, None])
    selector = (
        (offset[:, :, None] == jnp.arange(ACC, dtype=jnp.int32)[None, None, :])
        & writable[:, :, None]
    ).astype(jnp.bfloat16)
    placed = jnp.einsum(
        "rca,xrad->xrcd", selector, chosen, preferred_element_type=jnp.float32
    ).astype(jnp.bfloat16)
    new_cache = jnp.where(writable[None, :, :, None], placed, cache)
    return (attn_out, new_cache)


def solution(mesh):
    return jax.shard_map(
        local,
        mesh=mesh,
        in_specs=(
            P(None, "tp"),
            P(None, None, "seq", "tp"),
            P(None, "seq", "tp"),
            P("tp", "seq"),
            P(),
            P(),
            P(),
            P(),
        ),
        out_specs=(P("tp", "seq"), P(None, None, "seq", "tp")),
        check_vma=False,
    )
```

profile of v0, /device:TPU:0, one launch (start us, length us, event | category | flops | bytes accessed | tf_op | source)
XLA Modules:
  0.0 676.2 jit_solution(16713751382238479600)
XLA Ops:
  8.1 6.0 fusion.71
  14.8 38.0 %while.33 = (s32[]{:T(128)}, f32[4,4,64,1,8]{2,1,0,4,3:T(4,128)S(1)}, f32[4,4,64,1,8]{2,4,3,1,0:T(8,128)S(1)}, f32[4,4,64,1,8,128]{5,4,2,1,0,3:T(8,128)}, pred[4...) while((s32[]{:T(128)}, ...), condition=%wide.region_3.4_spmd, body=%wide.region_0.3_spmd.sunk | while | flops 1096806400 | bytes 32101996 | solution.py:120
  14.9 2.7 fusion.90
  17.6 3.0 fusion.91
  20.6 1.6 copy_dynamic-update-slice_fusion.5
  22.2 2.0 bitcast_reduce_fusion.2
  24.4 2.7 fusion.90
  27.1 3.0 fusion.91
  30.1 1.6 copy_dynamic-update-slice_fusion.5
  31.7 2.0 bitcast_reduce_fusion.2
  33.9 2.7 fusion.90
  36.6 3.0 fusion.91
  41.2 2.0 bitcast_reduce_fusion.2
  43.4 2.7 fusion.90
  46.1 3.0 fusion.91
  50.7 2.0 bitcast_reduce_fusion.2
  52.8 4.9 all_gather_reshape.11
  60.9 2.7 fusion.37
  63.5 1.7 fusion.39
  65.5 29.0 %all_gather.15 = bf16[2,1024,128]{2,1,0:T(8,128)(2,1)S(1)} all-gather(bf16[2,64,128]{2,1,0:T(8,128)(2,1)S(1)} %copy-done.7), channel_id=1, replica_groups=mesh['seq'=16,'tp'=8] {'seq'}, dimensions={1}, use_global_device_ids=true | all-gather | bytes 557056 | tf_op jit(solution)/shard_map/all_gather | solution.py:127
  95.3 2.1 fusion.24
  100.6 2.8 copy.71
  103.4 23.8 %all_gather.13 = f32[16,1024,8]{1,2,0:T(8,128)S(1)} all-gather(f32[1,1024,8]{1,2,0:T(8,128)} %all_gather_reshape.10), channel_id=1, replica_groups=mesh['seq'=16,'tp'=8] {'seq'}, dimensions={0}, use_global_device_ids=true | all-gather | bytes 557056 | tf_op jit(solution)/shard_map/all_gather | solution.py:13
  127.2 22.2 %all_gather.12 = f32[16,1024,8]{1,2,0:T(8,128)S(1)} all-gather(f32[1,1024,8]{1,2,0:T(8,128)} %all_gather_reshape.9), channel_id=1, replica_groups=mesh['seq'=16,'tp'=8] {'seq'}, dimensions={0}, use_global_device_ids=true | all-gather | bytes 557056 | tf_op jit(solution)/shard_map/all_gather | solution.py:13
  149.4 4.3 fusion.73
  153.7 253.1 %all-gather.2.cloned.1.call-done = f32[16,1024,1024]{2,1,0:T(8,128)} async-done(((f32[1,1024,1024]{2,1,0:T(8,128)}), f32[16,1024,1024]{2,1,0:T(8,128)}) %all-gather.2.cloned.1.call-update) | async-done | bytes 67108880 | tf_op jit(solution)/shard_map/all_gather | solution.py:13
  406.8 4.8 slice_bitcast_fusion
  411.6 207.2 %while.34 = (s32[]{:T(128)}, f32[1024,8]{0,1:T(8,128)S(1)}, f32[1024,8]{0,1:T(8,128)S(1)}, f32[1024,1024]{1,0:T(8,128)}, f32[16,1024,8]{1,2,0:T(8,128)S(1)}, /*i...) while((s32[]{:T(128)}, f32[1024,8]{0,1:T(8,128)S(1)}, ...), condition=%wide.region_5.6_spmd, body=%wide.region_4.5_spmd.sunk | while | flops 3194885 | bytes 46596272 | solution.py:19
  411.8 2.6 mul.191
  416.8 8.6 %fusion.93 = f32[1024,1024]{1,0:T(8,128)} fusion(f32[128,8,8,128]{3,2,1,0:T(8,128)S(1)} %bitcast.239, f32[1024,1024]{1,0:T(8,128)} %get-tuple-element.461, f32[128,8,8,128]{3,2,1,0:T(8,128)S(1)} %bitcast.240, f32[16,1024,1024]{2,1,0:T(8,128)} %get-tuple-element.474, s32[]{:T(128)S(6)} %select_n.68), kind=kLoop, calls=%fused_computation.27.clone.1 | loop fusion | flops 3145728 | bytes 20971524 | tf_op jit(solution)/shard_map/while/body/eval_jaxpr/add | solution.py:58
  425.6 2.6 mul.191
  430.6 8.6 %fusion.93 = f32[1024,1024]{1,0:T(8,128)} fusion(f32[128,8,8,128]{3,2,1,0:T(8,128)S(1)} %bitcast.239, f32[1024,1024]{1,0:T(8,128)} %get-tuple-element.461, f32[128,8,8,128]{3,2,1,0:T(8,128)S(1)} %bitcast.240, f32[16,1024,1024]{2,1,0:T(8,128)} %get-tuple-element.474, s32[]{:T(128)S(6)} %select_n.68), kind=kLoop, calls=%fused_computation.27.clone.1 | loop fusion | flops 3145728 | bytes 20971524 | tf_op jit(solution)/shard_map/while/body/eval_jaxpr/add | solution.py:58
  439.5 2.6 mul.191
  444.4 8.6 %fusion.93 = f32[1024,1024]{1,0:T(8,128)} fusion(f32[128,8,8,128]{3,2,1,0:T(8,128)S(1)} %bitcast.239, f32[1024,1024]{1,0:T(8,128)} %get-tuple-element.461, f32[128,8,8,128]{3,2,1,0:T(8,128)S(1)} %bitcast.240, f32[16,1024,1024]{2,1,0:T(8,128)} %get-tuple-element.474, s32[]{:T(128)S(6)} %select_n.68), kind=kLoop, calls=%fused_computation.27.clone.1 | loop fusion | flops 3145728 | bytes 20971524 | tf_op jit(solution)/shard_map/while/body/eval_jaxpr/add | solution.py:58
  453.3 2.6 mul.191
  458.2 8.6 %fusion.93 = f32[1024,1024]{1,0:T(8,128)} fusion(f32[128,8,8,128]{3,2,1,0:T(8,128)S(1)} %bitcast.239, f32[1024,1024]{1,0:T(8,128)} %get-tuple-element.461, f32[128,8,8,128]{3,2,1,0:T(8,128)S(1)} %bitcast.240, f32[16,1024,1024]{2,1,0:T(8,128)} %get-tuple-element.474, s32[]{:T(128)S(6)} %select_n.68), kind=kLoop, calls=%fused_computation.27.clone.1 | loop fusion | flops 3145728 | bytes 20971524 | tf_op jit(solution)/shard_map/while/body/eval_jaxpr/add | solution.py:58
  467.1 2.6 mul.191
  472.0 8.6 %fusion.93 = f32[1024,1024]{1,0:T(8,128)} fusion(f32[128,8,8,128]{3,2,1,0:T(8,128)S(1)} %bitcast.239, f32[1024,1024]{1,0:T(8,128)} %get-tuple-element.461, f32[128,8,8,128]{3,2,1,0:T(8,128)S(1)} %bitcast.240, f32[16,1024,1024]{2,1,0:T(8,128)} %get-tuple-element.474, s32[]{:T(128)S(6)} %select_n.68), kind=kLoop, calls=%fused_computation.27.clone.1 | loop fusion | flops 3145728 | bytes 20971524 | tf_op jit(solution)/shard_map/while/body/eval_jaxpr/add | solution.py:58
  480.9 2.6 mul.191
  485.9 8.6 %fusion.93 = f32[1024,1024]{1,0:T(8,128)} fusion(f32[128,8,8,128]{3,2,1,0:T(8,128)S(1)} %bitcast.239, f32[1024,1024]{1,0:T(8,128)} %get-tuple-element.461, f32[128,8,8,128]{3,2,1,0:T(8,128)S(1)} %bitcast.240, f32[16,1024,1024]{2,1,0:T(8,128)} %get-tuple-element.474, s32[]{:T(128)S(6)} %select_n.68), kind=kLoop, calls=%fused_computation.27.clone.1 | loop fusion | flops 3145728 | bytes 20971524 | tf_op jit(solution)/shard_map/while/body/eval_jaxpr/add | solution.py:58
  494.7 2.6 mul.191
  499.7 8.6 %fusion.93 = f32[1024,1024]{1,0:T(8,128)} fusion(f32[128,8,8,128]{3,2,1,0:T(8,128)S(1)} %bitcast.239, f32[1024,1024]{1,0:T(8,128)} %get-tuple-element.461, f32[128,8,8,128]{3,2,1,0:T(8,128)S(1)} %bitcast.240, f32[16,1024,1024]{2,1,0:T(8,128)} %get-tuple-element.474, s32[]{:T(128)S(6)} %select_n.68), kind=kLoop, calls=%fused_computation.27.clone.1 | loop fusion | flops 3145728 | bytes 20971524 | tf_op jit(solution)/shard_map/while/body/eval_jaxpr/add | solution.py:58
  508.5 2.6 mul.191
  513.5 8.6 %fusion.93 = f32[1024,1024]{1,0:T(8,128)} fusion(f32[128,8,8,128]{3,2,1,0:T(8,128)S(1)} %bitcast.239, f32[1024,1024]{1,0:T(8,128)} %get-tuple-element.461, f32[128,8,8,128]{3,2,1,0:T(8,128)S(1)} %bitcast.240, f32[16,1024,1024]{2,1,0:T(8,128)} %get-tuple-element.474, s32[]{:T(128)S(6)} %select_n.68), kind=kLoop, calls=%fused_computation.27.clone.1 | loop fusion | flops 3145728 | bytes 20971524 | tf_op jit(solution)/shard_map/while/body/eval_jaxpr/add | solution.py:58
  522.3 2.6 mul.191
  527.3 8.6 %fusion.93 = f32[1024,1024]{1,0:T(8,128)} fusion(f32[128,8,8,128]{3,2,1,0:T(8,128)S(1)} %bitcast.239, f32[1024,1024]{1,0:T(8,128)} %get-tuple-element.461, f32[128,8,8,128]{3,2,1,0:T(8,128)S(1)} %bitcast.240, f32[16,1024,1024]{2,1,0:T(8,128)} %get-tuple-element.474, s32[]{:T(128)S(6)} %select_n.68), kind=kLoop, calls=%fused_computation.27.clone.1 | loop fusion | flops 3145728 | bytes 20971524 | tf_op jit(solution)/shard_map/while/body/eval_jaxpr/add | solution.py:58
  536.1 2.6 mul.191
  541.1 8.6 %fusion.93 = f32[1024,1024]{1,0:T(8,128)} fusion(f32[128,8,8,128]{3,2,1,0:T(8,128)S(1)} %bitcast.239, f32[1024,1024]{1,0:T(8,128)} %get-tuple-element.461, f32[128,8,8,128]{3,2,1,0:T(8,128)S(1)} %bitcast.240, f32[16,1024,1024]{2,1,0:T(8,128)} %get-tuple-element.474, s32[]{:T(128)S(6)} %select_n.68), kind=kLoop, calls=%fused_computation.27.clone.1 | loop fusion | flops 3145728 | bytes 20971524 | tf_op jit(solution)/shard_map/while/body/eval_jaxpr/add | solution.py:58
  550.0 2.6 mul.191
  554.9 8.6 %fusion.93 = f32[1024,1024]{1,0:T(8,128)} fusion(f32[128,8,8,128]{3,2,1,0:T(8,128)S(1)} %bitcast.239, f32[1024,1024]{1,0:T(8,128)} %get-tuple-element.461, f32[128,8,8,128]{3,2,1,0:T(8,128)S(1)} %bitcast.240, f32[16,1024,1024]{2,1,0:T(8,128)} %get-tuple-element.474, s32[]{:T(128)S(6)} %select_n.68), kind=kLoop, calls=%fused_computation.27.clone.1 | loop fusion | flops 3145728 | bytes 20971524 | tf_op jit(solution)/shard_map/while/body/eval_jaxpr/add | solution.py:58
  563.8 2.6 mul.191
  568.7 8.6 %fusion.93 = f32[1024,1024]{1,0:T(8,128)} fusion(f32[128,8,8,128]{3,2,1,0:T(8,128)S(1)} %bitcast.239, f32[1024,1024]{1,0:T(8,128)} %get-tuple-element.461, f32[128,8,8,128]{3,2,1,0:T(8,128)S(1)} %bitcast.240, f32[16,1024,1024]{2,1,0:T(8,128)} %get-tuple-element.474, s32[]{:T(128)S(6)} %select_n.68), kind=kLoop, calls=%fused_computation.27.clone.1 | loop fusion | flops 3145728 | bytes 20971524 | tf_op jit(solution)/shard_map/while/body/eval_jaxpr/add | solution.py:58
  577.6 2.6 mul.191
  582.5 8.6 %fusion.93 = f32[1024,1024]{1,0:T(8,128)} fusion(f32[128,8,8,128]{3,2,1,0:T(8,128)S(1)} %bitcast.239, f32[1024,1024]{1,0:T(8,128)} %get-tuple-element.461, f32[128,8,8,128]{3,2,1,0:T(8,128)S(1)} %bitcast.240, f32[16,1024,1024]{2,1,0:T(8,128)} %get-tuple-element.474, s32[]{:T(128)S(6)} %select_n.68), kind=kLoop, calls=%fused_computation.27.clone.1 | loop fusion | flops 3145728 | bytes 20971524 | tf_op jit(solution)/shard_map/while/body/eval_jaxpr/add | solution.py:58
  591.4 2.6 mul.191
  596.4 8.6 %fusion.93 = f32[1024,1024]{1,0:T(8,128)} fusion(f32[128,8,8,128]{3,2,1,0:T(8,128)S(1)} %bitcast.239, f32[1024,1024]{1,0:T(8,128)} %get-tuple-element.461, f32[128,8,8,128]{3,2,1,0:T(8,128)S(1)} %bitcast.240, f32[16,1024,1024]{2,1,0:T(8,128)} %get-tuple-element.474, s32[]{:T(128)S(6)} %select_n.68), kind=kLoop, calls=%fused_computation.27.clone.1 | loop fusion | flops 3145728 | bytes 20971524 | tf_op jit(solution)/shard_map/while/body/eval_jaxpr/add | solution.py:58
  605.2 2.6 mul.191
  610.2 8.6 %fusion.93 = f32[1024,1024]{1,0:T(8,128)} fusion(f32[128,8,8,128]{3,2,1,0:T(8,128)S(1)} %bitcast.239, f32[1024,1024]{1,0:T(8,128)} %get-tuple-element.461, f32[128,8,8,128]{3,2,1,0:T(8,128)S(1)} %bitcast.240, f32[16,1024,1024]{2,1,0:T(8,128)} %get-tuple-element.474, s32[]{:T(128)S(6)} %select_n.68), kind=kLoop, calls=%fused_computation.27.clone.1 | loop fusion | flops 3145728 | bytes 20971524 | tf_op jit(solution)/shard_map/while/body/eval_jaxpr/add | solution.py:58
  624.0 3.9 fusion.32
  628.0 12.3 %copy.77 = bf16[2,16,1024,128]{2,3,0,1:T(8,128)(2,1)} copy(bf16[2,16,1024,128]{3,2,1,0:T(8,128)(2,1)} %param.13) | data formatting | bytes 16777216 | tf_op args[1]
  640.5 7.2 %bitcast_select_fusion.1 = bf16[2,16,1024,128]{2,3,0,1:T(8,128)(2,1)} fusion(bf16[2,16,1024,128]{2,3,0,1:T(8,128)(2,1)} %copy.77, pred[16,1024]{1,0:T(8,128)(4,1)S(1)} %compare_and_fusion, bf16[2,16,64,128]{3,2,1,0:T(8,128)(2,1)S(1)} %bitcast.244, s32[16,1024]{1,0:T(8,128)S(1)} %broadcast_subtract_fusion, s32[16,8]{1,0:T(8,128)S(1)} %copy.75), kind=kOutput, calls=%fused_computation.35 | convolution fusion | flops 79994880 | bytes 17383936 | tf_op jit(solution)/shard_map/rca,xrad->xrcd/dot_general | solution.py:143
  647.7 11.9 %copy.78 = bf16[2,16,1024,128]{3,2,1,0:T(8,128)(2,1)} copy(bf16[2,16,1024,128]{2,3,0,1:T(8,128)(2,1)} %bitcast_select_fusion.1) | data formatting | bytes 16777216
  659.6 8.2 %reduce-scatter.2.cloned.1.call-done = f32[128,512]{1,0:T(8,128)} async-done(((f32[1024,512]{1,0:T(8,128)}), f32[128,512]{1,0:T(8,128)}) %reduce-scatter.2.cloned.1.call-update) | async-done | bytes 262160 | tf_op jit(solution)/shard_map/reduce_scatter | solution.py:131
  667.7 1.6 convert_element_type.60
  (165 shorter events, 56.9 us)
Async XLA Ops:
  7.2 615.7 %copy-start = (bf16[1024,512]{1,0:T(8,128)(2,1)S(1)}, bf16[1024,512]{1,0:T(8,128)(2,1)}, u32[]{:S(2)}) copy-start(bf16[1024,512]{1,0:T(8,128)(2,1)} %param.15) | copy-start | bytes 3145732
  7.2 399.6 %all-gather.2.cloned.1.call-start = ((), (), s32[]{:S(2)}) async-start(), calls=%async_computation.1 | async-start | bytes 71303168 | tf_op jit(solution)/shard_map/all_gather | solution.py:13
  8.1 6.0 copy-start.6
  57.7 1.6 copy-start.11
  57.7 7.8 %copy-start.7 = (bf16[2,64,128]{2,1,0:T(8,128)(2,1)S(1)}, bf16[2,64,128]{2,1,0:T(8,128)(2,1)}, u32[]{:S(2)}) copy-start(bf16[2,64,128]{2,1,0:T(8,128)(2,1)} %param.14) | copy-start | bytes 98308
  57.7 610.0 %reduce-scatter.2.cloned.1.call-start = ((), (), s32[]{:S(2)}) async-start(), calls=%async_computation.2 | async-start | bytes 2359296 | tf_op jit(solution)/shard_map/reduce_scatter | solution.py:131
  94.5 0.8 copy-start.3
  414.6 2.2 copy-start.1
  428.4 2.2 copy-start.1
  442.2 2.2 copy-start.1
  456.0 2.2 copy-start.1
  469.9 2.2 copy-start.1
  483.7 2.2 copy-start.1
  497.5 2.2 copy-start.1
  511.3 2.2 copy-start.1
  525.1 2.2 copy-start.1
  538.9 2.2 copy-start.1
  552.7 2.2 copy-start.1
  566.5 2.2 copy-start.1
  580.4 2.2 copy-start.1
  594.2 2.2 copy-start.1
  608.0 2.2 copy-start.1
  620.6 2.3 copy-start.2
  620.6 3.5 copy-start.5
  627.9 12.4 %copy-start.9 = (s32[16,8]{0,1:T(8,128)S(1)}, s32[16,8]{0,1:T(8,128)}, u32[]{:S(2)}) copy-start(s32[16,8]{0,1:T(8,128)} %param.18) | copy-start | bytes 1540
  628.0 12.4 %copy-start.8 = (s32[16]{0:T(128)S(1)}, s32[16]{0:T(128)}, u32[]{:S(2)}) copy-start(s32[16]{0:T(128)} %param.16) | copy-start | bytes 196
  628.0 12.4 %copy-start.10 = (s32[16]{0:T(128)S(1)}, s32[16]{0:T(128)}, u32[]{:S(2)}) copy-start(s32[16]{0:T(128)} %param.19) | copy-start | bytes 196
  628.0 12.6 %copy-start.4 = (bf16[2,1024,128]{2,1,0:T(8,128)(2,1)S(1)}, bf16[2,1024,128]{2,1,0:T(8,128)(2,1)}, u32[]{:S(2)}) copy-start(bf16[2,1024,128]{2,1,0:T(8,128)(2,1)} %copy-done.3) | copy-start | bytes 1572868
Sparse Core Ops, SparseCore 0:
  57.8 348.9 all-gather.1
  628.1 39.6 reduce-scatter.1
where the time goes:
time: 678 us; the launch traced here: 676 us
  waiting for transfers between devices  261 us (38%)
  other arithmetic  141 us (21%)
  local copies, waits for them, and re-layouts  137 us (20%)
  blocking collectives  74.9 us (11%)
  matrix products  46.3 us (7%)
  between operations  14.3 us (2%)
    all_gather x1, waiting for transfers between devices, merged_2(): everything = jax.tree.map(lambda part: lax.all_gather(part, axis), array)  253 us
    add x15, other arithmetic, join_flat(): former[2].reshape(row_count, head_count, -1) * weight_former[..., None]  129 us
    all_gather x2, blocking collectives, merged_2(): everything = jax.tree.map(lambda part: lax.all_gather(part, axis), array)  46 us
    mul x16, local copies, waits for them, and re-layouts, join_flat(): latter[2].reshape(row_count, head_count, -1) * weight_latter[..., None]  39.8 us
    all_gather x1, blocking collectives, local(): drafts = lax.all_gather(draft_kv, 'seq', axis=1, tiled=True)  29 us
    unnamed x26, local copies, waits for them, and re-layouts  26.8 us
    mul x16, local copies, waits for them, and re-layouts, join_flat(): former[2].reshape(row_count, head_count, -1) * weight_former[..., None]  18.2 us
    dot_general x5, matrix products, partial_block(): jnp.einsum('nqkgp,npke->nqkge', weights.astype(jnp.bfloat16), value_rows,...  16.4 us
  transfers between devices with their start and end apart: 2, of which 2 were waited for; matrix products, arithmetic and copies ran while one was open for 8% of the time, Pallas kernels for 0%

commit v1 on v0

--- a/solution.py
+++ b/solution.py
@@ -124,7 +124,9 @@
     peak_score = peak_score.reshape(token_rows, heads_local)
     denominator = denominator.reshape(token_rows, heads_local)
     weighted = weighted.reshape(token_rows, heads_local * HEAD)
-    drafts = lax.all_gather(draft_kv, "seq", axis=1, tiled=True)
+    drafts = jnp.concatenate(
+        lax.all_to_all(jnp.stack([draft_kv] * lax.axis_size("seq")), "seq", 0, 0), axis=1
+    )
     merged = merged_2((peak_score, denominator, weighted), "seq", join_flat)
     attended = finish(queries, drafts, parents, merged, kv_local)
     chosen = select_rows(drafts, path)

time: 678 us -> 690 us (1.018)
  blocking collectives: 74.9 us -> 52.4 us
  other arithmetic: 141 us -> 153 us
  waiting for transfers between devices: 261 us -> 273 us
  starting transfers between devices: 0.08 us -> 8.25 us
    all_gather x1 -> x0, blocking collectives: 29 us -> none  [local(): drafts = lax.all_gather(draft_kv, 'seq', axis=1, tiled=True)]
    all_gather x1, waiting for transfers between devices: 253 us -> 265 us  [merged_2(): everything = jax.tree.map(lambda part: lax.all_gather(part, axis), array)]
    add x16, other arithmetic: 0.4 us -> 12.2 us  [join_flat(): former[1] * weight_former + latter[1] * weight_latter]
    all_to_all x0 -> x1, starting transfers between devices: none -> 8.18 us  [local(): lax.all_to_all(jnp.stack([draft_kv] * lax.axis_size('seq')), 'seq', 0, 0)]
    unnamed x26 -> x28, local copies, waits for them, and re-layouts: 26.8 us -> 28.3 us
  transfers between devices with their start and end apart: 2 -> 3, of which waited for: 2 -> 2; matrix products, arithmetic and copies ran while one was open for 8% -> 7% of each run, Pallas kernels for 0% -> 0%
where the time goes in v1:
time: 690 us; the launch traced here: 687 us
  waiting for transfers between devices  273 us (40%)
  other arithmetic  153 us (22%)
  local copies, waits for them, and re-layouts  139 us (20%)
  blocking collectives  52.4 us (8%)
  matrix products  46.6 us (7%)
  between operations  14.3 us (2%)
  starting transfers between devices  8.25 us (1%)
    all_gather x1, waiting for transfers between devices, merged_2(): everything = jax.tree.map(lambda part: lax.all_gather(part, axis), array)  265 us
    add x15, other arithmetic, join_flat(): former[2].reshape(row_count, head_count, -1) * weight_former[..., None]  129 us
    all_gather x2, blocking collectives, merged_2(): everything = jax.tree.map(lambda part: lax.all_gather(part, axis), array)  52.4 us
    mul x16, local copies, waits for them, and re-layouts, join_flat(): latter[2].reshape(row_count, head_count, -1) * weight_latter[..., None]  40.3 us
    unnamed x28, local copies, waits for them, and re-layouts  28.3 us
    mul x16, local copies, waits for them, and re-layouts, join_flat(): former[2].reshape(row_count, head_count, -1) * weight_former[..., None]  18.2 us
    dot_general x5, matrix products, partial_block(): jnp.einsum('nqkgp,npke->nqkge', weights.astype(jnp.bfloat16), value_rows,...  16.4 us
    while x30, local copies, waits for them, and re-layouts  15.7 us
  transfers between devices with their start and end apart: 3, of which 2 were waited for; matrix products, arithmetic and copies ran while one was open for 7% of the time, Pallas kernels for 0%

profile of v1, /device:TPU:0, one launch (start us, length us, event | category | flops | bytes accessed | tf_op | source)
XLA Modules:
  0.0 687.4 jit_solution(9212866516709958332)
XLA Ops:
  8.1 6.0 fusion.72
  14.8 38.0 %while.33 = (s32[]{:T(128)}, f32[4,4,64,1,8]{2,1,0,4,3:T(4,128)S(1)}, f32[4,4,64,1,8]{2,4,3,1,0:T(8,128)S(1)}, f32[4,4,64,1,8,128]{5,4,2,1,0,3:T(8,128)}, pred[4...) while((s32[]{:T(128)}, ...), condition=%wide.region_3.4_spmd, body=%wide.region_0.3_spmd.sunk | while | flops 1096806400 | bytes 32101996 | solution.py:120
  14.9 2.7 fusion.87
  17.6 3.0 fusion.88
  22.2 2.0 bitcast_reduce_fusion.2
  24.4 2.7 fusion.87
  27.1 3.0 fusion.88
  31.7 2.0 bitcast_reduce_fusion.2
  33.9 2.7 fusion.87
  36.6 3.0 fusion.88
  39.6 1.6 copy_dynamic-update-slice_fusion.5
  41.2 2.0 bitcast_reduce_fusion.2
  43.4 2.7 fusion.87
  46.1 3.0 fusion.88
  49.1 1.6 copy_dynamic-update-slice_fusion.5
  50.7 2.0 bitcast_reduce_fusion.2
  52.8 4.9 all_gather_reshape.11
  59.4 8.2 %all-to-all-start = ((bf16[16,2,64,128]{3,2,1,0:T(8,128)(2,1)}), bf16[16,2,64,128]{3,2,1,0:T(8,128)(2,1)}, u32[]{:S(2)}, u32[]{:S(2)}) async-start(bf16[16,2,64,128]{3,2,1,0:T(8,128)(2,1)} %stack.2), calls=%async_computation | async-start | bytes 1048576 | tf_op jit(solution)/shard_map/all_to_all | solution.py:128
  69.4 2.6 fusion.37
  71.9 1.9 fusion.39
  73.8 28.8 %all_gather.10 = f32[16,1024,8]{1,2,0:T(8,128)S(1)} all-gather(f32[1,1024,8]{1,2,0:T(8,128)S(1)} %all_gather_reshape.10), channel_id=1, replica_groups=mesh['seq'=16,'tp'=8] {'seq'}, dimensions={0}, use_global_device_ids=true | all-gather | bytes 557056 | tf_op jit(solution)/shard_map/all_gather | solution.py:13
  103.8 23.6 %all_gather.9 = f32[16,1024,8]{1,2,0:T(8,128)S(1)} all-gather(f32[1,1024,8]{1,2,0:T(8,128)S(1)} %all_gather_reshape.9), channel_id=1, replica_groups=mesh['seq'=16,'tp'=8] {'seq'}, dimensions={0}, use_global_device_ids=true | all-gather | bytes 557056 | tf_op jit(solution)/shard_map/all_gather | solution.py:13
  129.3 2.1 fusion.24
  133.2 3.0 copy.74
  136.2 4.3 fusion.46
  140.4 265.3 %all-gather.2.cloned.1.call-done = f32[16,1024,1024]{2,1,0:T(8,128)} async-done(((f32[1,1024,1024]{2,1,0:T(8,128)}), f32[16,1024,1024]{2,1,0:T(8,128)}) %all-gather.2.cloned.1.call-update) | async-done | bytes 67108880 | tf_op jit(solution)/shard_map/all_gather | solution.py:13
  405.8 4.8 slice_bitcast_fusion
  410.6 219.5 %while.34 = (s32[]{:T(128)}, f32[1024,8]{0,1:T(8,128)S(1)}, f32[1024,8]{0,1:T(8,128)S(1)}, f32[1024,1024]{1,0:T(8,128)}, f32[16,1024,8]{1,2,0:T(8,128)}, /*index...) while((s32[]{:T(128)}, f32[1024,8]{0,1:T(8,128)S(1)}, ...), condition=%wide.region_5.6_spmd, body=%wide.region_4.5_spmd.sunk | while | flops 3194885 | bytes 46596272 | solution.py:19
  411.6 2.6 mul.191
  416.6 8.6 %fusion.90 = f32[1024,1024]{1,0:T(8,128)} fusion(f32[128,8,8,128]{3,2,1,0:T(8,128)S(1)} %bitcast.247, f32[1024,1024]{1,0:T(8,128)} %get-tuple-element.459, f32[128,8,8,128]{3,2,1,0:T(8,128)S(1)} %bitcast.248, f32[16,1024,1024]{2,1,0:T(8,128)} %get-tuple-element.472, s32[]{:T(128)S(6)} %select_n.68), kind=kLoop, calls=%fused_computation.27.clone.1 | loop fusion | flops 3145728 | bytes 20971524 | tf_op jit(solution)/shard_map/while/body/eval_jaxpr/add | solution.py:58
  426.2 2.6 mul.191
  431.2 8.6 %fusion.90 = f32[1024,1024]{1,0:T(8,128)} fusion(f32[128,8,8,128]{3,2,1,0:T(8,128)S(1)} %bitcast.247, f32[1024,1024]{1,0:T(8,128)} %get-tuple-element.459, f32[128,8,8,128]{3,2,1,0:T(8,128)S(1)} %bitcast.248, f32[16,1024,1024]{2,1,0:T(8,128)} %get-tuple-element.472, s32[]{:T(128)S(6)} %select_n.68), kind=kLoop, calls=%fused_computation.27.clone.1 | loop fusion | flops 3145728 | bytes 20971524 | tf_op jit(solution)/shard_map/while/body/eval_jaxpr/add | solution.py:58
  440.9 2.6 mul.191
  445.9 8.6 %fusion.90 = f32[1024,1024]{1,0:T(8,128)} fusion(f32[128,8,8,128]{3,2,1,0:T(8,128)S(1)} %bitcast.247, f32[1024,1024]{1,0:T(8,128)} %get-tuple-element.459, f32[128,8,8,128]{3,2,1,0:T(8,128)S(1)} %bitcast.248, f32[16,1024,1024]{2,1,0:T(8,128)} %get-tuple-element.472, s32[]{:T(128)S(6)} %select_n.68), kind=kLoop, calls=%fused_computation.27.clone.1 | loop fusion | flops 3145728 | bytes 20971524 | tf_op jit(solution)/shard_map/while/body/eval_jaxpr/add | solution.py:58
  455.5 2.6 mul.191
  460.5 8.6 %fusion.90 = f32[1024,1024]{1,0:T(8,128)} fusion(f32[128,8,8,128]{3,2,1,0:T(8,128)S(1)} %bitcast.247, f32[1024,1024]{1,0:T(8,128)} %get-tuple-element.459, f32[128,8,8,128]{3,2,1,0:T(8,128)S(1)} %bitcast.248, f32[16,1024,1024]{2,1,0:T(8,128)} %get-tuple-element.472, s32[]{:T(128)S(6)} %select_n.68), kind=kLoop, calls=%fused_computation.27.clone.1 | loop fusion | flops 3145728 | bytes 20971524 | tf_op jit(solution)/shard_map/while/body/eval_jaxpr/add | solution.py:58
  470.1 2.6 mul.191
  475.1 8.6 %fusion.90 = f32[1024,1024]{1,0:T(8,128)} fusion(f32[128,8,8,128]{3,2,1,0:T(8,128)S(1)} %bitcast.247, f32[1024,1024]{1,0:T(8,128)} %get-tuple-element.459, f32[128,8,8,128]{3,2,1,0:T(8,128)S(1)} %bitcast.248, f32[16,1024,1024]{2,1,0:T(8,128)} %get-tuple-element.472, s32[]{:T(128)S(6)} %select_n.68), kind=kLoop, calls=%fused_computation.27.clone.1 | loop fusion | flops 3145728 | bytes 20971524 | tf_op jit(solution)/shard_map/while/body/eval_jaxpr/add | solution.py:58
  484.8 2.6 mul.191
  489.8 8.6 %fusion.90 = f32[1024,1024]{1,0:T(8,128)} fusion(f32[128,8,8,128]{3,2,1,0:T(8,128)S(1)} %bitcast.247, f32[1024,1024]{1,0:T(8,128)} %get-tuple-element.459, f32[128,8,8,128]{3,2,1,0:T(8,128)S(1)} %bitcast.248, f32[16,1024,1024]{2,1,0:T(8,128)} %get-tuple-element.472, s32[]{:T(128)S(6)} %select_n.68), kind=kLoop, calls=%fused_computation.27.clone.1 | loop fusion | flops 3145728 | bytes 20971524 | tf_op jit(solution)/shard_map/while/body/eval_jaxpr/add | solution.py:58
  499.4 2.6 mul.191
  504.4 8.6 %fusion.90 = f32[1024,1024]{1,0:T(8,128)} fusion(f32[128,8,8,128]{3,2,1,0:T(8,128)S(1)} %bitcast.247, f32[1024,1024]{1,0:T(8,128)} %get-tuple-element.459, f32[128,8,8,128]{3,2,1,0:T(8,128)S(1)} %bitcast.248, f32[16,1024,1024]{2,1,0:T(8,128)} %get-tuple-element.472, s32[]{:T(128)S(6)} %select_n.68), kind=kLoop, calls=%fused_computation.27.clone.1 | loop fusion | flops 3145728 | bytes 20971524 | tf_op jit(solution)/shard_map/while/body/eval_jaxpr/add | solution.py:58
  514.0 2.6 mul.191
  519.0 8.6 %fusion.90 = f32[1024,1024]{1,0:T(8,128)} fusion(f32[128,8,8,128]{3,2,1,0:T(8,128)S(1)} %bitcast.247, f32[1024,1024]{1,0:T(8,128)} %get-tuple-element.459, f32[128,8,8,128]{3,2,1,0:T(8,128)S(1)} %bitcast.248, f32[16,1024,1024]{2,1,0:T(8,128)} %get-tuple-element.472, s32[]{:T(128)S(6)} %select_n.68), kind=kLoop, calls=%fused_computation.27.clone.1 | loop fusion | flops 3145728 | bytes 20971524 | tf_op jit(solution)/shard_map/while/body/eval_jaxpr/add | solution.py:58
  528.7 2.6 mul.191
  533.7 8.6 %fusion.90 = f32[1024,1024]{1,0:T(8,128)} fusion(f32[128,8,8,128]{3,2,1,0:T(8,128)S(1)} %bitcast.247, f32[1024,1024]{1,0:T(8,128)} %get-tuple-element.459, f32[128,8,8,128]{3,2,1,0:T(8,128)S(1)} %bitcast.248, f32[16,1024,1024]{2,1,0:T(8,128)} %get-tuple-element.472, s32[]{:T(128)S(6)} %select_n.68), kind=kLoop, calls=%fused_computation.27.clone.1 | loop fusion | flops 3145728 | bytes 20971524 | tf_op jit(solution)/shard_map/while/body/eval_jaxpr/add | solution.py:58
  543.3 2.6 mul.191
  548.3 8.6 %fusion.90 = f32[1024,1024]{1,0:T(8,128)} fusion(f32[128,8,8,128]{3,2,1,0:T(8,128)S(1)} %bitcast.247, f32[1024,1024]{1,0:T(8,128)} %get-tuple-element.459, f32[128,8,8,128]{3,2,1,0:T(8,128)S(1)} %bitcast.248, f32[16,1024,1024]{2,1,0:T(8,128)} %get-tuple-element.472, s32[]{:T(128)S(6)} %select_n.68), kind=kLoop, calls=%fused_computation.27.clone.1 | loop fusion | flops 3145728 | bytes 20971524 | tf_op jit(solution)/shard_map/while/body/eval_jaxpr/add | solution.py:58
  557.9 2.6 mul.191
  562.9 8.6 %fusion.90 = f32[1024,1024]{1,0:T(8,128)} fusion(f32[128,8,8,128]{3,2,1,0:T(8,128)S(1)} %bitcast.247, f32[1024,1024]{1,0:T(8,128)} %get-tuple-element.459, f32[128,8,8,128]{3,2,1,0:T(8,128)S(1)} %bitcast.248, f32[16,1024,1024]{2,1,0:T(8,128)} %get-tuple-element.472, s32[]{:T(128)S(6)} %select_n.68), kind=kLoop, calls=%fused_computation.27.clone.1 | loop fusion | flops 3145728 | bytes 20971524 | tf_op jit(solution)/shard_map/while/body/eval_jaxpr/add | solution.py:58
  572.6 2.6 mul.191
  577.6 8.6 %fusion.90 = f32[1024,1024]{1,0:T(8,128)} fusion(f32[128,8,8,128]{3,2,1,0:T(8,128)S(1)} %bitcast.247, f32[1024,1024]{1,0:T(8,128)} %get-tuple-element.459, f32[128,8,8,128]{3,2,1,0:T(8,128)S(1)} %bitcast.248, f32[16,1024,1024]{2,1,0:T(8,128)} %get-tuple-element.472, s32[]{:T(128)S(6)} %select_n.68), kind=kLoop, calls=%fused_computation.27.clone.1 | loop fusion | flops 3145728 | bytes 20971524 | tf_op jit(solution)/shard_map/while/body/eval_jaxpr/add | solution.py:58
  587.2 2.6 mul.191
  592.2 8.6 %fusion.90 = f32[1024,1024]{1,0:T(8,128)} fusion(f32[128,8,8,128]{3,2,1,0:T(8,128)S(1)} %bitcast.247, f32[1024,1024]{1,0:T(8,128)} %get-tuple-element.459, f32[128,8,8,128]{3,2,1,0:T(8,128)S(1)} %bitcast.248, f32[16,1024,1024]{2,1,0:T(8,128)} %get-tuple-element.472, s32[]{:T(128)S(6)} %select_n.68), kind=kLoop, calls=%fused_computation.27.clone.1 | loop fusion | flops 3145728 | bytes 20971524 | tf_op jit(solution)/shard_map/while/body/eval_jaxpr/add | solution.py:58
  601.8 2.6 mul.191
  606.8 8.6 %fusion.90 = f32[1024,1024]{1,0:T(8,128)} fusion(f32[128,8,8,128]{3,2,1,0:T(8,128)S(1)} %bitcast.247, f32[1024,1024]{1,0:T(8,128)} %get-tuple-element.459, f32[128,8,8,128]{3,2,1,0:T(8,128)S(1)} %bitcast.248, f32[16,1024,1024]{2,1,0:T(8,128)} %get-tuple-element.472, s32[]{:T(128)S(6)} %select_n.68), kind=kLoop, calls=%fused_computation.27.clone.1 | loop fusion | flops 3145728 | bytes 20971524 | tf_op jit(solution)/shard_map/while/body/eval_jaxpr/add | solution.py:58
  616.5 2.6 mul.191
  621.5 8.6 %fusion.90 = f32[1024,1024]{1,0:T(8,128)} fusion(f32[128,8,8,128]{3,2,1,0:T(8,128)S(1)} %bitcast.247, f32[1024,1024]{1,0:T(8,128)} %get-tuple-element.459, f32[128,8,8,128]{3,2,1,0:T(8,128)S(1)} %bitcast.248, f32[16,1024,1024]{2,1,0:T(8,128)} %get-tuple-element.472, s32[]{:T(128)S(6)} %select_n.68), kind=kLoop, calls=%fused_computation.27.clone.1 | loop fusion | flops 3145728 | bytes 20971524 | tf_op jit(solution)/shard_map/while/body/eval_jaxpr/add | solution.py:58
  635.3 3.9 fusion.32
  639.3 12.3 %copy.80 = bf16[2,16,1024,128]{2,3,0,1:T(8,128)(2,1)} copy(bf16[2,16,1024,128]{3,2,1,0:T(8,128)(2,1)} %param.13) | data formatting | bytes 16777216 | tf_op args[1]
  651.8 7.4 %bitcast_select_fusion.1 = bf16[2,16,1024,128]{2,3,0,1:T(8,128)(2,1)} fusion(bf16[2,16,1024,128]{2,3,0,1:T(8,128)(2,1)} %copy.80, pred[16,1024]{1,0:T(8,128)(4,1)S(1)} %compare_and_fusion, bf16[16,2,64,128]{3,2,1,0:T(8,128)(2,1)} %all-to-all-done, s32[16,1024]{1,0:T(8,128)S(1)} %broadcast_subtract_fusion, s32[16,8]{1,0:T(8,128)S(1)} %copy.78), kind=kOutput, calls=%fused_computation.35 | convolution fusion | flops 79994880 | bytes 17383936 | tf_op jit(solution)/shard_map/rca,xrad->xrcd/dot_general | solution.py:145
  659.2 11.9 %copy.81 = bf16[2,16,1024,128]{3,2,1,0:T(8,128)(2,1)} copy(bf16[2,16,1024,128]{2,3,0,1:T(8,128)(2,1)} %bitcast_select_fusion.1) | data formatting | bytes 16777216
  671.0 7.9 %reduce-scatter.2.cloned.1.call-done = f32[128,512]{1,0:T(8,128)} async-done(((f32[1024,512]{1,0:T(8,128)}), f32[128,512]{1,0:T(8,128)}) %reduce-scatter.2.cloned.1.call-update) | async-done | bytes 262160 | tf_op jit(solution)/shard_map/reduce_scatter | solution.py:133
  679.0 1.6 convert_element_type.60
  (169 shorter events, 69.5 us)
Async XLA Ops:
  7.2 627.0 %copy-start = (bf16[1024,512]{1,0:T(8,128)(2,1)S(1)}, bf16[1024,512]{1,0:T(8,128)(2,1)}, u32[]{:S(2)}) copy-start(bf16[1024,512]{1,0:T(8,128)(2,1)} %param.15) | copy-start | bytes 3145732
  7.2 398.6 %all-gather.2.cloned.1.call-start = ((), (), s32[]{:S(2)}) async-start(), calls=%async_computation.2 | async-start | bytes 71303168 | tf_op jit(solution)/shard_map/all_gather | solution.py:13
  8.1 6.0 copy-start.5
  57.7 0.8 copy-start.8
  57.7 10.1 %copy-start.12 = (s32[16,64]{1,0:T(8,128)S(1)}, s32[16,64]{1,0:T(8,128)}, u32[]{:S(2)}) copy-start(s32[16,64]{1,0:T(8,128)} %param.17) | copy-start | bytes 12292
  59.4 68.8 %all-to-all-start = ((bf16[16,2,64,128]{3,2,1,0:T(8,128)(2,1)}), bf16[16,2,64,128]{3,2,1,0:T(8,128)(2,1)}, u32[]{:S(2)}, u32[]{:S(2)}) async-start(bf16[16,2,64,128]{3,2,1,0:T(8,128)(2,1)} %stack.2), calls=%async_computation | async-start | bytes 1048576 | tf_op jit(solution)/shard_map/all_to_all | solution.py:128
  67.6 611.4 %reduce-scatter.2.cloned.1.call-start = ((), (), s32[]{:S(2)}) async-start(), calls=%async_computation.3 | async-start | bytes 2359296 | tf_op jit(solution)/shard_map/reduce_scatter | solution.py:133
  102.6 0.8 copy-start.6
  127.4 0.8 copy-start.7
  129.3 2.2 copy-start.4
  414.4 2.2 copy-start.1
  429.0 2.2 copy-start.1
  443.7 2.2 copy-start.1
  458.3 2.2 copy-start.1
  472.9 2.2 copy-start.1
  487.6 2.2 copy-start.1
  502.2 2.2 copy-start.1
  516.8 2.2 copy-start.1
  531.5 2.2 copy-start.1
  546.1 2.2 copy-start.1
  560.7 2.2 copy-start.1
  575.4 2.2 copy-start.1
  590.0 2.2 copy-start.1
  604.6 2.2 copy-start.1
  619.3 2.2 copy-start.1
  631.9 2.3 copy-start.2
  631.9 3.5 copy-start.3
  639.2 12.3 %copy-start.10 = (s32[16,8]{0,1:T(8,128)S(1)}, s32[16,8]{0,1:T(8,128)}, u32[]{:S(2)}) copy-start(s32[16,8]{0,1:T(8,128)} %param.18) | copy-start | bytes 1540
  639.2 12.4 %copy-start.9 = (s32[16]{0:T(128)S(1)}, s32[16]{0:T(128)}, u32[]{:S(2)}) copy-start(s32[16]{0:T(128)} %param.16) | copy-start | bytes 196
  639.3 12.3 %copy-start.11 = (s32[16]{0:T(128)S(1)}, s32[16]{0:T(128)}, u32[]{:S(2)}) copy-start(s32[16]{0:T(128)} %param.19) | copy-start | bytes 196
Sparse Core Ops, SparseCore 0:
  57.9 347.8 all-gather.1
  639.4 39.5 reduce-scatter.1
